TPU v7x, 32 devices: a whole 2x2x4 slice. The times are simulated.
32 devices in a mesh: lat: 4 (over y, x), lon: 8 (over z, core).
Axes of the slice: x: 2, y: 2, z: 4, core: 2. Of those that a mesh axis runs over, the one named last changes fastest.
Arguments:
- queries: bfloat16 [64, 64, 768], P('lat', 'lon'), may hold values from -8 to 8
- key_vectors: bfloat16 [64, 64, 768], P('lat', 'lon'), may hold values from -8 to 8
- value_vectors: bfloat16 [64, 64, 768], P('lat', 'lon'), may hold values from -12 to 12
- upstream: bfloat16 [64, 64, 768], P('lat', 'lon'), may hold values from -6 to 6
- w_out: bfloat16 [768, 768], replicated, may hold values from -0.21875 to 0.21875
- neighbours: int32 [8, 8, 4], replicated, may hold values from 0 to 63, as said below
- counts: int32 [8, 8], replicated, may hold values from 2 to 4, as said below
Outputs:
- mixed_out: bfloat16 [64, 64, 768], P('lat', 'lon')
- q_grad: bfloat16 [64, 64, 768], P('lat', 'lon')
- k_grad: bfloat16 [64, 64, 768], P('lat', 'lon')
- v_grad: bfloat16 [64, 64, 768], P('lat', 'lon')
- w_grad: float32 [768, 768], replicated
Inputs may be any that keep to these rules, and one draw needn't show every extreme that they name: `neighbours`: entry s of block (i, j) names a block i2 * 8 + j2 with i2 within one of i and j2 within one of j around the longitude circle; slot 0 names the block itself, the entries of slots below counts[i, j] are distinct, and the slots at or beyond counts[i, j] name the block itself. `counts`: every block outside the first and the last row of blocks has 4.
All inputs are finite; a program needn't handle non-finite values.
Results may differ from a plain program's by a relative error of at most 0.03.
Values may be sent and summed in bfloat16 or wider, within the bound.
No kernel may reach another device: no remote copies, remote signals or barrier semaphores. Data moves between devices by JAX's collectives and lax.ppermute only.
A program may use at most 64 MiB of HBM per device.

v0:
```python
import math
import jax
import jax.numpy as jnp
from jax import lax
from jax.sharding import PartitionSpec as P

HEADS = 12
HEAD_DIM = 64
BLK = 8
SLOTS = 4


def padded_2(value, sides, width):
    for axis, dim in sides:
        peers, length = (lax.axis_size(axis), value.shape[dim])
        up = [(i, (i + 1) % peers) for i in range(peers)]
        down = [(j, i) for i, j in up]
        last = lax.slice_in_dim(value, length - width, length, axis=dim)
        leading = lax.slice_in_dim(value, 0, width, axis=dim)
        before = lax.ppermute(last, axis, up)
        after = lax.ppermute(leading, axis, down)
        value = jnp.concatenate([before, value, after], axis=dim)
    return value


def to_blocks(token_grid):
    lat_rows, lon_cols, feat_width = token_grid.shape
    block_tiles = token_grid.reshape(
        lat_rows // BLK, BLK, lon_cols // BLK, BLK, feat_width
    ).transpose(0, 2, 1, 3, 4)
    return block_tiles.reshape(lat_rows // BLK * (lon_cols // BLK), BLK * BLK, feat_width)


def from_blocks(block_tiles, lat_blocks, lon_blocks):
    feat_width = block_tiles.shape[-1]
    token_grid = block_tiles.reshape(lat_blocks, lon_blocks, BLK, BLK, feat_width).transpose(
        0, 2, 1, 3, 4
    )
    return token_grid.reshape(lat_blocks * BLK, lon_blocks * BLK, feat_width)


def split_heads(block_tiles):
    return block_tiles.reshape(block_tiles.shape[0], block_tiles.shape[1], HEADS, HEAD_DIM)


def slot_places(
    neighbours,
    counts,
    first_lat,
    first_lon,
    grid_rows,
    grid_cols,
    anchor_lat,
    anchor_lon,
    pad_rows,
    pad_cols,
):
    total_lat = neighbours.shape[0]
    total_lon = neighbours.shape[1]
    block_lat = first_lat + jnp.arange(grid_rows, dtype=jnp.int32)
    block_lon = (first_lon + jnp.arange(grid_cols, dtype=jnp.int32)) % total_lon
    inside = (block_lat >= 0) & (block_lat < total_lat)
    safe_lat = jnp.clip(block_lat, 0, total_lat - 1)
    slot_table = jnp.take(jnp.take(neighbours, safe_lat, axis=0), block_lon, axis=1)
    slot_limit = jnp.take(jnp.take(counts, safe_lat, axis=0), block_lon, axis=1)
    slot_ids = jnp.arange(SLOTS, dtype=jnp.int32)
    rel_lat = slot_table // total_lon - anchor_lat
    rel_lon = (slot_table % total_lon - anchor_lon) % total_lon
    usable = (slot_ids[None, None, :] < slot_limit[:, :, None]) & inside[:, None, None]
    usable = usable & (rel_lat >= 0) & (rel_lat < pad_rows) & (rel_lon < pad_cols)
    key_place = jnp.where(usable, rel_lat * pad_cols + rel_lon, 0)
    return (
        key_place.reshape(grid_rows * grid_cols, SLOTS),
        usable.reshape(grid_rows * grid_cols, SLOTS),
    )


def gather_sets(padded_tiles, key_place):
    picked = jnp.take(padded_tiles, key_place.reshape(-1), axis=0)
    return picked.reshape(key_place.shape[0], SLOTS * BLK * BLK, padded_tiles.shape[-1])


def masked_scores(query_tiles, key_sets, key_valid):
    raw = jnp.einsum(
        "nqhd,nkhd->nhqk",
        split_heads(query_tiles),
        split_heads(key_sets),
        preferred_element_type=jnp.float32,
    )
    raw = raw * (1.0 / math.sqrt(HEAD_DIM))
    return jnp.where(key_valid[:, None, None, :], raw, -jnp.inf)


def forward_core(query_tiles, key_sets, value_sets, key_valid):
    masked = masked_scores(query_tiles, key_sets, key_valid)
    row_top = jnp.max(masked, axis=-1, keepdims=True)
    exp_total = jnp.sum(jnp.exp(masked - row_top), axis=-1, keepdims=True)
    log_total = row_top + jnp.log(exp_total)
    attn_probs = jnp.exp(masked - log_total)
    probs_low = attn_probs.astype(jnp.bfloat16)
    mixed_heads = jnp.einsum(
        "nhqk,nkhd->nqhd", probs_low, split_heads(value_sets), preferred_element_type=jnp.float32
    )
    attended = mixed_heads.astype(jnp.bfloat16).reshape(query_tiles.shape)
    return (attended, attn_probs, probs_low, log_total[..., 0])


def head_delta(d_att, attended):
    product = d_att.astype(jnp.float32) * attended.astype(jnp.float32)
    return jnp.sum(split_heads(product), axis=-1).transpose(0, 2, 1)


def backward_scores(attn_probs, d_att, row_delta, value_sets):
    dprobs = jnp.einsum(
        "nqhd,nkhd->nhqk",
        split_heads(d_att),
        split_heads(value_sets),
        preferred_element_type=jnp.float32,
    )
    return (attn_probs * (dprobs - row_delta[..., None]) * (1.0 / math.sqrt(HEAD_DIM))).astype(
        jnp.bfloat16
    )


def grad_queries(dscores, key_sets):
    summed = jnp.einsum(
        "nhqk,nkhd->nqhd", dscores, split_heads(key_sets), preferred_element_type=jnp.float32
    )
    return summed.astype(jnp.bfloat16).reshape(summed.shape[0], summed.shape[1], -1)


def contract_keys(weights_low, block_tiles):
    summed = jnp.einsum(
        "nhqk,nqhd->nkhd", weights_low, split_heads(block_tiles), preferred_element_type=jnp.float32
    )
    return summed.reshape(summed.shape[0], summed.shape[1], -1)


def add_into(contrib, key_place, usable, pad_count):
    flat_place = key_place.reshape(-1)
    feat_width = contrib.shape[-1]
    flat_terms = contrib.reshape(flat_place.shape[0], BLK * BLK * feat_width)
    flat_terms = jnp.where(usable.reshape(-1)[:, None], flat_terms, 0.0)
    summed = (
        jnp.zeros((pad_count, BLK * BLK * feat_width), jnp.float32).at[flat_place].add(flat_terms)
    )
    return summed.reshape(pad_count, BLK * BLK, feat_width)


def fold_joint(extended, lat_rows, lon_cols):
    low_lat = lat_rows + 3 * BLK
    low_lon = lon_cols + 3 * BLK
    interior = extended[:, 2 * BLK : 2 * BLK + lat_rows, 2 * BLK : 2 * BLK + lon_cols]
    interior = interior.at[:, :BLK, :].add(extended[:, :BLK, 2 * BLK : 2 * BLK + lon_cols])
    interior = interior.at[:, lat_rows - BLK :, :].add(
        extended[:, low_lat:, 2 * BLK : 2 * BLK + lon_cols]
    )
    interior = interior.at[:, :, :BLK].add(extended[:, 2 * BLK : 2 * BLK + lat_rows, :BLK])
    interior = interior.at[:, :, lon_cols - BLK :].add(
        extended[:, 2 * BLK : 2 * BLK + lat_rows, low_lon:]
    )
    interior = interior.at[:, :BLK, :BLK].add(extended[:, :BLK, :BLK])
    interior = interior.at[:, :BLK, lon_cols - BLK :].add(extended[:, :BLK, low_lon:])
    interior = interior.at[:, lat_rows - BLK :, :BLK].add(extended[:, low_lat:, :BLK])
    return interior.at[:, lat_rows - BLK :, lon_cols - BLK :].add(extended[:, low_lat:, low_lon:])


def on_device(queries, key_vectors, value_vectors, upstream, w_out, neighbours, counts):
    lat_rows, lon_cols, feat_width = queries.shape
    lat_blocks = lat_rows // BLK
    lon_blocks = lon_cols // BLK
    pad_rows = lat_blocks + 2
    pad_cols = lon_blocks + 2
    pad_count = pad_rows * pad_cols
    inner_count = BLK * BLK
    tokens_all = lat_rows * lon_cols * lax.axis_size("lat") * lax.axis_size("lon")
    first_lat = lax.axis_index("lat") * lat_blocks
    first_lon = lax.axis_index("lon") * lon_blocks
    stacked = jnp.stack((key_vectors, value_vectors))
    padded = padded_2(stacked, (("lat", 1), ("lon", 2)), BLK)
    key_tiles = to_blocks(padded[0])
    value_tiles = to_blocks(padded[1])
    own_place, own_usable = slot_places(
        neighbours,
        counts,
        first_lat,
        first_lon,
        lat_blocks,
        lon_blocks,
        first_lat - 1,
        first_lon - 1,
        pad_rows,
        pad_cols,
    )
    query_tiles = to_blocks(queries)
    key_sets = gather_sets(key_tiles, own_place)
    value_sets = gather_sets(value_tiles, own_place)
    key_valid = jnp.repeat(own_usable, inner_count, axis=1)
    attended, attn_probs, probs_low, log_total = forward_core(
        query_tiles, key_sets, value_sets, key_valid
    )
    flat_att = attended.reshape(-1, feat_width)
    mixed_flat = jnp.dot(flat_att, w_out, preferred_element_type=jnp.float32).astype(jnp.bfloat16)
    grad_tiles = to_blocks(upstream)
    flat_grad = grad_tiles.reshape(-1, feat_width)
    local_weight = lax.dot_general(
        flat_att, flat_grad, (((0,), (0,)), ((), ())), preferred_element_type=jnp.float32
    )
    w_grad = lax.psum(local_weight, ("lat", "lon")) / math.sqrt(tokens_all)
    d_att = lax.dot_general(
        flat_grad, w_out, (((1,), (1,)), ((), ())), preferred_element_type=jnp.float32
    )
    d_att = d_att.astype(jnp.bfloat16).reshape(attended.shape)
    row_delta = head_delta(d_att, attended)
    dscores = backward_scores(attn_probs, d_att, row_delta, value_sets)
    query_grad = grad_queries(dscores, key_sets)
    key_contrib = contract_keys(dscores, query_tiles)
    value_contrib = contract_keys(probs_low, d_att)
    key_pad = from_blocks(
        add_into(key_contrib, own_place, own_usable, pad_count), pad_rows, pad_cols
    )
    value_pad = from_blocks(
        add_into(value_contrib, own_place, own_usable, pad_count), pad_rows, pad_cols
    )
    pad_terms = jnp.stack((key_pad, value_pad))
    extended = padded_2(pad_terms.astype(jnp.bfloat16), (("lat", 1), ("lon", 2)), BLK).astype(
        pad_terms.dtype
    )
    folded = fold_joint(extended, lat_rows, lon_cols)
    key_grad = folded[0].astype(jnp.bfloat16)
    value_grad = folded[1].astype(jnp.bfloat16)
    mixed_out = from_blocks(mixed_flat.reshape(attended.shape), lat_blocks, lon_blocks)
    q_grad = from_blocks(query_grad, lat_blocks, lon_blocks)
    return (mixed_out, q_grad, key_grad, value_grad, w_grad)


def solution(mesh):
    return jax.shard_map(
        on_device,
        mesh=mesh,
        in_specs=(
            P("lat", "lon", None),
            P("lat", "lon", None),
            P("lat", "lon", None),
            P("lat", "lon", None),
            P(),
            P(),
            P(),
        ),
        out_specs=(
            P("lat", "lon", None),
            P("lat", "lon", None),
            P("lat", "lon", None),
            P("lat", "lon", None),
            P(),
        ),
        check_vma=False,
    )
```

profile of v0, /device:TPU:0, one launch (start us, length us, event | category | flops | bytes accessed | tf_op | source)
XLA Modules:
  0.0 270.1 jit_solution(14660080153096011954)
XLA Ops:
  7.2 1.2 fusion.18
  8.4 4.0 %collective-permute-start.1 = (bf16[2,8,8,768]{3,2,1,0:T(8,128)(2,1)S(1)}, bf16[2,8,8,768]{3,2,1,0:T(8,128)(2,1)S(1)}, u32[]{:S(2)}, u32[]{:S(2)}) collective-permute-start(bf16[2,8,8,768]{3,2,1,0:T(8,128)(2,1)S(1)} %get-tuple-element.152), channel_id=1, source_target_pairs={{8,0},{16,8},{24,16},{0,24},{9,1},{17,9},{25,17},{1,25},{10,2},{18... | collective-permute-start | bytes 589832 | tf_op jit(solution)/shard_map/ppermute | solution.py:21
  12.5 1.3 gather_fusion.1
  13.8 1.2 gather_fusion
  15.5 1.5 convolution_convert_fusion.2
  17.7 4.1 %collective-permute-done = bf16[2,8,8,768]{3,2,1,0:T(8,128)(2,1)S(1)} collective-permute-done((bf16[2,8,8,768]{3,2,1,0:T(8,128)(2,1)S(1)}, bf16[2,8,8,768]{3,2,1,0:T(8,128)(2,1)S(1)}, u32[]{:S(2)}, u32[]{:S(2)}) %collective-permute-start) | collective-permute-done | bytes 196640 | tf_op jit(solution)/shard_map/ppermute | solution.py:20
  22.8 2.2 collective-permute-start.3
  25.7 1.1 copy.42
  26.8 1.3 reshape_reshape_transpose_reshape.7
  28.1 1.1 copy.45
  30.0 12.1 %collective-permute-done.3 = bf16[2,32,8,768]{3,2,1,0:T(8,128)(2,1)S(1)} collective-permute-done((bf16[2,32,8,768]{3,2,1,0:T(8,128)(2,1)}, bf16[2,32,8,768]{3,2,1,0:T(8,128)(2,1)S(1)}, u32[]{:S(2)}, u32[]{:S(2)}) %collective-permute-start.3) | collective-permute-done | bytes 786464 | tf_op jit(solution)/shard_map/ppermute | solution.py:21
  42.1 3.0 %collective-permute-done.2 = bf16[2,32,8,768]{3,2,1,0:T(8,128)(2,1)} collective-permute-done((bf16[2,32,8,768]{3,2,1,0:T(8,128)(2,1)}, bf16[2,32,8,768]{3,2,1,0:T(8,128)(2,1)}, u32[]{:S(2)}, u32[]{:S(2)}) %collective-permute-start.2) | collective-permute-done | bytes 786464 | tf_op jit(solution)/shard_map/ppermute | solution.py:20
  45.1 1.3 pad_maximum_fusion
  46.7 1.5 gather_fusion.3
  48.2 1.5 gather_fusion.2
  49.7 2.5 broadcast_select_fusion.2
  52.2 2.7 %reshape.774 = bf16[2,256,12,64]{3,2,1,0:T(8,128)(2,1)S(1)} reshape(bf16[8,64,768]{2,1,0:T(8,128)(2,1)} %get-tuple-element.156) | data formatting | bytes 1572864 | tf_op jit(solution)/shard_map/reshape;reshape | solution.py:43
  54.9 2.1 copy.37
  57.1 2.7 %reshape.775 = bf16[2,256,12,64]{3,2,1,0:T(8,128)(2,1)S(1)} reshape(bf16[8,64,768]{2,1,0:T(8,128)(2,1)} %get-tuple-element.155) | data formatting | bytes 1572864 | tf_op jit(solution)/shard_map/reshape;reshape | solution.py:43
  59.8 2.1 copy.35
  62.0 1.8 bitcast_reduce_fusion
  65.5 1.3 multiply_reduce_fusion
  68.4 1.5 convolution_bitcast_fusion
  69.9 4.7 %copy.46 = f32[2,256,12,64]{3,2,1,0:T(8,128)} copy(f32[2,256,12,64]{1,3,2,0:T(8,128)} %convolution_bitcast_fusion) | data formatting | bytes 3145728 | tf_op jit(solution)/shard_map/nhqk,nqhd->nkhd/transpose | solution.py:133
  74.6 4.4 %reshape_reshape.37 = f32[8,49152]{1,0:T(8,128)} reshape(f32[2,256,12,64]{3,2,1,0:T(8,128)} %copy.46) | data formatting | bytes 3145728 | tf_op jit(solution)/shard_map/reshape;reshape | solution.py:142
  79.0 3.7 %copy.49 = f32[2,256,12,64]{3,2,1,0:T(8,128)} copy(f32[2,256,12,64]{1,3,2,0:T(8,128)S(1)} %convolution_bitcast_fusion.1) | data formatting | bytes 3145728 | tf_op jit(solution)/shard_map/nhqk,nqhd->nkhd/transpose | solution.py:133
  82.8 4.5 %reshape_reshape.39 = f32[8,49152]{1,0:T(8,128)} reshape(f32[2,256,12,64]{3,2,1,0:T(8,128)} %copy.49) | data formatting | bytes 3145728 | tf_op jit(solution)/shard_map/reshape;reshape | solution.py:142
  87.3 3.4 %broadcast_select_fusion.1 = (f32[8,49152]{1,0:T(8,128)}, f32[8,49152]{1,0:T(8,128)}) fusion(f32[8,49152]{1,0:T(8,128)S(1)} %copy-done.6, pred[8]{0:T(512)(128)(4,1)S(1)} %get-tuple-element.142, f32[8,49152]{1,0:T(8,128)} %reshape_reshape.39), kind=kLoop, calls=%fused_computation.38 | loop fusion | flops 786432 | bytes 6291464 | tf_op jit(solution)/shard_map/jit(_where)/select_n | solution.py:143
  90.7 5.1 %scatter_custom_fusion.1 = f32[12,49152]{1,0:T(8,128)} fusion(s32[8]{0:T(128)} %fusion.33, f32[8,49152]{1,0:T(8,128)} %get-tuple-element.154, f32[]{:T(128)} %constant.347.clone.1), kind=kCustom, calls=%fused_computation.13 | custom fusion | flops 393216 | bytes 2359808 | tf_op jit(solution)/shard_map/scatter-add | solution.py:145
  95.7 2.0 convert.17
  98.3 4.9 %scatter_custom_fusion = f32[12,49152]{1,0:T(8,128)} fusion(s32[8]{0:T(128)} %fusion.33, f32[8,49152]{1,0:T(8,128)} %get-tuple-element.153, f32[]{:T(128)} %constant.347.clone.1), kind=kCustom, calls=%fused_computation.15 | custom fusion | flops 393216 | bytes 2359808 | tf_op jit(solution)/shard_map/scatter-add | solution.py:145
  103.2 2.0 convert.16
  105.8 1.1 pad_maximum_fusion.7
  106.9 1.4 collective-permute-start.5
  108.9 1.2 copy.38
  110.1 1.9 reshape_reshape.35
  112.0 2.9 %fusion.19 = f32[768,768]{1,0:T(8,128)} fusion(bf16[128,768]{0,1:T(8,128)(2,1)} %reshape_reshape.35, bf16[16,8,768]{2,1,0:T(8,128)(2,1)} %param.32), kind=kOutput, calls=%fused_computation.71 | convolution fusion | flops 150994944 | bytes 2752512 | tf_op jit(solution)/shard_map/dot_general | solution.py:206
  114.9 10.2 %collective-permute-done.5 = bf16[2,8,24,768]{3,2,1,0:T(8,128)(2,1)} collective-permute-done((bf16[2,8,24,768]{3,2,1,0:T(8,128)(2,1)}, bf16[2,8,24,768]{3,2,1,0:T(8,128)(2,1)}, u32[]{:S(2)}, u32[]{:S(2)}) %collective-permute-start.5) | collective-permute-done | bytes 589856 | tf_op jit(solution)/shard_map/ppermute | solution.py:21
  125.1 10.0 %collective-permute-done.4 = bf16[2,8,24,768]{3,2,1,0:T(8,128)(2,1)} collective-permute-done((bf16[2,8,24,768]{3,2,1,0:T(8,128)(2,1)}, bf16[2,8,24,768]{3,2,1,0:T(8,128)(2,1)}, u32[]{:S(2)}, u32[]{:S(2)}) %collective-permute-start.4) | collective-permute-done | bytes 589856 | tf_op jit(solution)/shard_map/ppermute | solution.py:20
  135.1 2.8 %pad_maximum_fusion.4 = (bf16[2,48,8,768]{3,2,1,0:T(8,128)(2,1)}, bf16[2,48,8,768]{3,2,1,0:T(8,128)(2,1)}) fusion(bf16[2,8,24,768]{3,2,1,0:T(8,128)(2,1)} %collective-permute-done.5, bf16[2,8,24,768]{3,2,1,0:T(8,128)(2,1)} %collective-permute-done.4, bf16[1,32,24,768]{3,2,1,0:T(8,128)(2,1)S(1)} %bitcast.90, bf16[1,32,24,768]{3,2,1,0:T(8,128)(2,1)S(1)} %bitcast.100), kind=kLoop, calls=%fused_computation.29 | loop fusion | flops 9437184 | bytes 5898240 | tf_op jit(solution)/shard_map/slice | solution.py:18
  137.9 4.1 %collective-permute-start.7 = (bf16[2,48,8,768]{3,2,1,0:T(8,128)(2,1)}, bf16[2,48,8,768]{3,2,1,0:T(8,128)(2,1)}, u32[]{:S(2)}, u32[]{:S(2)}) collective-permute-start(bf16[2,48,8,768]{3,2,1,0:T(8,128)(2,1)} %get-tuple-element.144), channel_id=1, source_target_pairs={{1,0},{2,1},{3,2},{4,3},{5,4},{6,5},{7,6},{0,7},{9,8},{10,9},{11,1... | collective-permute-start | bytes 3538952 | tf_op jit(solution)/shard_map/ppermute | solution.py:21
  142.0 1.1 fusion.9
  143.1 2.2 copy.44
  145.3 2.1 reshape_transpose_reshape_reshape.7
  147.4 2.0 fusion.10
  149.3 102.2 %all-reduce.2.cloned.1.call-done = f32[768,768]{1,0:T(8,128)} async-done(((f32[768,768]{1,0:T(8,128)}), f32[768,768]{1,0:T(8,128)}) %all-reduce.2.cloned.1.call-update) | async-done | bytes 2359312 | tf_op jit(solution)/shard_map/psum | solution.py:209
  251.6 3.2 %broadcast_multiply_fusion = f32[768,768]{1,0:T(8,128)} fusion(f32[768,768]{1,0:T(8,128)} %all-reduce.2.cloned.1.call-done), kind=kLoop, calls=%fused_computation.30 | loop fusion | flops 589824 | bytes 4718592 | tf_op jit(solution)/shard_map/div | solution.py:209
  256.9 1.3 convert_add_fusion
  (77 shorter events, 16.2 us)
Async XLA Ops:
  7.2 8.3 %copy-start = (bf16[768,768]{1,0:T(8,128)(2,1)S(1)}, bf16[768,768]{1,0:T(8,128)(2,1)}, u32[]{:S(2)}) copy-start(bf16[768,768]{1,0:T(8,128)(2,1)} %param.33) | copy-start | bytes 3538948
  7.2 14.6 %copy-start.9 = (bf16[16,8,768]{2,1,0:T(8,128)(2,1)S(1)}, bf16[16,8,768]{2,1,0:T(8,128)(2,1)}, u32[]{:S(2)}) copy-start(bf16[16,8,768]{2,1,0:T(8,128)(2,1)} %param.30) | copy-start | bytes 589828
  7.2 14.6 %copy-start.10 = (bf16[16,8,768]{2,1,0:T(8,128)(2,1)S(1)}, bf16[16,8,768]{2,1,0:T(8,128)(2,1)}, u32[]{:S(2)}) copy-start(bf16[16,8,768]{2,1,0:T(8,128)(2,1)} %param.31) | copy-start | bytes 589828
  7.2 244.4 %all-reduce.2.cloned.1.call-start = ((), (), s32[]{:S(2)}) async-start(), calls=%async_computation | async-start | bytes 4718592 | tf_op jit(solution)/shard_map/psum | solution.py:209
  8.4 9.3 %collective-permute-start.1 = (bf16[2,8,8,768]{3,2,1,0:T(8,128)(2,1)S(1)}, bf16[2,8,8,768]{3,2,1,0:T(8,128)(2,1)S(1)}, u32[]{:S(2)}, u32[]{:S(2)}) collective-permute-start(bf16[2,8,8,768]{3,2,1,0:T(8,128)(2,1)S(1)} %get-tuple-element.152), channel_id=1, source_target_pairs={{8,0},{16,8},{24,16},{0,24},{9,1},{17,9},{25,17},{1,25},{10,2},{18... | collective-permute-start | bytes 589832 | tf_op jit(solution)/shard_map/ppermute | solution.py:21
  12.4 9.4 %collective-permute-start = (bf16[2,8,8,768]{3,2,1,0:T(8,128)(2,1)S(1)}, bf16[2,8,8,768]{3,2,1,0:T(8,128)(2,1)S(1)}, u32[]{:S(2)}, u32[]{:S(2)}) collective-permute-start(bf16[2,8,8,768]{3,2,1,0:T(8,128)(2,1)S(1)} %get-tuple-element.151), channel_id=1, source_target_pairs={{0,8},{8,16},{16,24},{24,0},{1,9},{9,17},{17,25},{25,1},{2,10},{10... | collective-permute-start | bytes 589832 | tf_op jit(solution)/shard_map/ppermute | solution.py:20
  22.8 19.3 %collective-permute-start.3 = (bf16[2,32,8,768]{3,2,1,0:T(8,128)(2,1)}, bf16[2,32,8,768]{3,2,1,0:T(8,128)(2,1)S(1)}, u32[]{:S(2)}, u32[]{:S(2)}) collective-permute-start(bf16[2,32,8,768]{3,2,1,0:T(8,128)(2,1)} %pad_maximum_fusion.5), channel_id=1, source_target_pairs={{1,0},{2,1},{3,2},{4,3},{5,4},{6,5},{7,6},{0,7},{9,8},{10,9},{11,1... | collective-permute-start | bytes 2359304 | tf_op jit(solution)/shard_map/ppermute | solution.py:21
  24.9 20.1 %collective-permute-start.2 = (bf16[2,32,8,768]{3,2,1,0:T(8,128)(2,1)}, bf16[2,32,8,768]{3,2,1,0:T(8,128)(2,1)}, u32[]{:S(2)}, u32[]{:S(2)}) collective-permute-start(bf16[2,32,8,768]{3,2,1,0:T(8,128)(2,1)} %pad_maximum_fusion.5), channel_id=1, source_target_pairs={{0,1},{1,2},{2,3},{3,4},{4,5},{5,6},{6,7},{7,0},{8,9},{9,10},{10,1... | collective-permute-start | bytes 2359304 | tf_op jit(solution)/shard_map/ppermute | solution.py:20
  48.2 1.5 copy-start.8
  62.0 2.4 copy-start.5
  64.3 1.1 copy-start.3
  66.7 1.7 copy-start.7
  67.4 1.0 copy-start.1
  82.8 4.5 %copy-start.6 = (f32[8,49152]{1,0:T(8,128)S(1)}, f32[8,49152]{1,0:T(8,128)}, u32[]{:S(2)}) copy-start(f32[8,49152]{1,0:T(8,128)} %reshape_reshape.37) | copy-start | bytes 4718596
  105.7 3.2 %copy-start.11 = (bf16[2,64,12,64]{1,3,2,0:T(8,128)(2,1)S(1)}, bf16[2,64,12,64]{1,3,2,0:T(8,128)(2,1)}, u32[]{:S(2)}) copy-start(bf16[2,64,12,64]{1,3,2,0:T(8,128)(2,1)} %get-tuple-element.162) | copy-start | bytes 589828
  106.9 18.2 %collective-permute-start.5 = (bf16[2,8,24,768]{3,2,1,0:T(8,128)(2,1)}, bf16[2,8,24,768]{3,2,1,0:T(8,128)(2,1)}, u32[]{:S(2)}, u32[]{:S(2)}) collective-permute-start(bf16[2,8,24,768]{3,2,1,0:T(8,128)(2,1)} %get-tuple-element.146), channel_id=1, source_target_pairs={{8,0},{16,8},{24,16},{0,24},{9,1},{17,9},{25,17},{1,25},{10,2},{18... | collective-permute-start | bytes 1769480 | tf_op jit(solution)/shard_map/ppermute | solution.py:21
  108.3 26.7 %collective-permute-start.4 = (bf16[2,8,24,768]{3,2,1,0:T(8,128)(2,1)}, bf16[2,8,24,768]{3,2,1,0:T(8,128)(2,1)}, u32[]{:S(2)}, u32[]{:S(2)}) collective-permute-start(bf16[2,8,24,768]{3,2,1,0:T(8,128)(2,1)} %get-tuple-element.145), channel_id=1, source_target_pairs={{0,8},{8,16},{16,24},{24,0},{1,9},{9,17},{17,25},{25,1},{2,10},{10... | collective-permute-start | bytes 1769480 | tf_op jit(solution)/shard_map/ppermute | solution.py:20
  114.9 27.1 %copy-start.2 = (bf16[2,12,64,256]{3,2,1,0:T(8,128)(2,1)S(1)}, bf16[2,12,64,256]{3,2,1,0:T(8,128)(2,1)}, u32[]{:S(2)}) copy-start(bf16[2,12,64,256]{3,2,1,0:T(8,128)(2,1)} %copy-done.1) | copy-start | bytes 2359300
  114.9 27.1 %copy-start.4 = (bf16[2,256,12,64]{1,3,2,0:T(8,128)(2,1)S(1)}, bf16[2,256,12,64]{1,3,2,0:T(8,128)(2,1)}, u32[]{:S(2)}) copy-start(bf16[2,256,12,64]{1,3,2,0:T(8,128)(2,1)} %copy.35) | copy-start | bytes 2359300
  137.9 116.9 %collective-permute-start.7 = (bf16[2,48,8,768]{3,2,1,0:T(8,128)(2,1)}, bf16[2,48,8,768]{3,2,1,0:T(8,128)(2,1)}, u32[]{:S(2)}, u32[]{:S(2)}) collective-permute-start(bf16[2,48,8,768]{3,2,1,0:T(8,128)(2,1)} %get-tuple-element.144), channel_id=1, source_target_pairs={{1,0},{2,1},{3,2},{4,3},{5,4},{6,5},{7,6},{0,7},{9,8},{10,9},{11,1... | collective-permute-start | bytes 3538952 | tf_op jit(solution)/shard_map/ppermute | solution.py:21
  142.0 112.8 %collective-permute-start.6 = (bf16[2,48,8,768]{3,2,1,0:T(8,128)(2,1)}, bf16[2,48,8,768]{3,2,1,0:T(8,128)(2,1)}, u32[]{:S(2)}, u32[]{:S(2)}) collective-permute-start(bf16[2,48,8,768]{3,2,1,0:T(8,128)(2,1)} %get-tuple-element.143), channel_id=1, source_target_pairs={{0,1},{1,2},{2,3},{3,4},{4,5},{5,6},{6,7},{7,0},{8,9},{9,10},{10,1... | collective-permute-start | bytes 3538952 | tf_op jit(solution)/shard_map/ppermute | solution.py:20
Sparse Core Ops, SparseCore 0:
  115.0 136.5 all-reduce.1
where the time goes:
time: 271 us; the launch traced here: 270 us
  waiting for transfers between devices  142 us (52%)
  local copies, waits for them, and re-layouts  48.2 us (18%)
  other arithmetic  39.8 us (15%)
  between operations  14.4 us (5%)
  matrix products  13.1 us (5%)
  starting transfers between devices  12.4 us (5%)
    psum x1, waiting for transfers between devices, on_device(): w_grad = lax.psum(local_weight, ('lat', 'lon')) / math.sqrt(tokens_all)  102 us
    ppermute x4, waiting for transfers between devices, padded_2(): after = lax.ppermute(leading, axis, down)  23 us
    ppermute x4, waiting for transfers between devices, padded_2(): before = lax.ppermute(last, axis, up)  17.1 us
    another operation x8, local copies, waits for them, and re-layouts, split_heads(): block_tiles.reshape(block_tiles.shape[0], block_tiles.shape[1], HEADS, HE...  13.6 us
    ppermute x4, starting transfers between devices, padded_2(): after = lax.ppermute(leading, axis, down)  11.7 us
    scatter-add x2, other arithmetic, add_into(): jnp.zeros((pad_count, BLK * BLK * feat_width), jnp.float32).at[flat_place]  9.96 us
    another operation x2, local copies, waits for them, and re-layouts, add_into(): flat_terms = contrib.reshape(flat_place.shape[0], BLK * BLK * feat_width)  8.94 us
    transpose x2, local copies, waits for them, and re-layouts, contract_keys(): jnp.einsum('nhqk,nqhd->nkhd', weights_low, split_heads(block_tiles), pref...  8.46 us
  transfers between devices with their start and end apart: 9, of which 7 were waited for; matrix products, arithmetic and copies ran while one was open for 11% of the time, Pallas kernels for 0%

commit v1 on v0

--- a/solution.py
+++ b/solution.py
@@ -3,11 +3,18 @@
 import jax.numpy as jnp
 from jax import lax
 from jax.sharding import PartitionSpec as P
+from jax.lax import psum
 
 HEADS = 12
 HEAD_DIM = 64
 BLK = 8
 SLOTS = 4
+
+
+def edit_leaves(message, link_axis, axis_key):
+    for p in (link_axis, axis_key):
+        message = psum(message, p)
+    return message
 
 
 def padded_2(value, sides, width):
@@ -206,7 +213,7 @@
     local_weight = lax.dot_general(
         flat_att, flat_grad, (((0,), (0,)), ((), ())), preferred_element_type=jnp.float32
     )
-    w_grad = lax.psum(local_weight, ("lat", "lon")) / math.sqrt(tokens_all)
+    w_grad = edit_leaves(local_weight, "lon", "lat") / math.sqrt(tokens_all)
     d_att = lax.dot_general(
         flat_grad, w_out, (((1,), (1,)), ((), ())), preferred_element_type=jnp.float32
     )

time: 271 us -> 281 us (1.037)
  waiting for transfers between devices: 142 us -> 151 us
    psum x1 -> x2, waiting for transfers between devices: 102 us -> 115 us  [edit_leaves(): message = psum(message, p)]
  transfers between devices with their start and end apart: 9 -> 10, of which waited for: 7 -> 8; matrix products, arithmetic and copies ran while one was open for 11% -> 13% of each run, Pallas kernels for 0% -> 0%
where the time goes in v1:
time: 281 us; the launch traced here: 280 us
  waiting for transfers between devices  151 us (54%)
  local copies, waits for them, and re-layouts  48.1 us (17%)
  other arithmetic  39.9 us (14%)
  matrix products  14.6 us (5%)
  between operations  14.4 us (5%)
  starting transfers between devices  11.8 us (4%)
    psum x2, waiting for transfers between devices, edit_leaves(): message = psum(message, p)  115 us
    ppermute x4, waiting for transfers between devices, padded_2(): after = lax.ppermute(leading, axis, down)  21.2 us
    ppermute x4, waiting for transfers between devices, padded_2(): before = lax.ppermute(last, axis, up)  14.6 us
    another operation x8, local copies, waits for them, and re-layouts, split_heads(): block_tiles.reshape(block_tiles.shape[0], block_tiles.shape[1], HEADS, HE...  13.6 us
    ppermute x4, starting transfers between devices, padded_2(): after = lax.ppermute(leading, axis, down)  11.1 us
    scatter-add x2, other arithmetic, add_into(): jnp.zeros((pad_count, BLK * BLK * feat_width), jnp.float32).at[flat_place]  9.98 us
    another operation x2, local copies, waits for them, and re-layouts, add_into(): flat_terms = contrib.reshape(flat_place.shape[0], BLK * BLK * feat_width)  8.94 us
    transpose x2, local copies, waits for them, and re-layouts, contract_keys(): jnp.einsum('nhqk,nqhd->nkhd', weights_low, split_heads(block_tiles), pref...  8.46 us
  transfers between devices with their start and end apart: 10, of which 8 were waited for; matrix products, arithmetic and copies ran while one was open for 13% of the time, Pallas kernels for 0%

profile of v1, /device:TPU:0, one launch (start us, length us, event | category | flops | bytes accessed | tf_op | source)
XLA Modules:
  0.0 279.8 jit_solution(17389488359421213702)
XLA Ops:
  7.2 1.2 fusion.18
  8.4 4.0 %collective-permute-start.1 = (bf16[2,8,8,768]{3,2,1,0:T(8,128)(2,1)S(1)}, bf16[2,8,8,768]{3,2,1,0:T(8,128)(2,1)S(1)}, u32[]{:S(2)}, u32[]{:S(2)}) collective-permute-start(bf16[2,8,8,768]{3,2,1,0:T(8,128)(2,1)S(1)} %get-tuple-element.152), channel_id=1, source_target_pairs={{8,0},{16,8},{24,16},{0,24},{9,1},{17,9},{25,17},{1,25},{10,2},{18... | collective-permute-start | bytes 589832 | tf_op jit(solution)/shard_map/ppermute | solution.py:28
  12.5 1.3 gather_fusion.1
  13.8 1.2 gather_fusion
  15.5 1.5 convolution_convert_fusion.2
  17.7 4.1 %collective-permute-done = bf16[2,8,8,768]{3,2,1,0:T(8,128)(2,1)S(1)} collective-permute-done((bf16[2,8,8,768]{3,2,1,0:T(8,128)(2,1)S(1)}, bf16[2,8,8,768]{3,2,1,0:T(8,128)(2,1)S(1)}, u32[]{:S(2)}, u32[]{:S(2)}) %collective-permute-start) | collective-permute-done | bytes 196640 | tf_op jit(solution)/shard_map/ppermute | solution.py:27
  22.8 2.2 collective-permute-start.3
  25.7 1.1 copy.42
  26.8 1.3 reshape_reshape_transpose_reshape.7
  28.1 1.1 copy.45
  30.0 12.1 %collective-permute-done.3 = bf16[2,32,8,768]{3,2,1,0:T(8,128)(2,1)S(1)} collective-permute-done((bf16[2,32,8,768]{3,2,1,0:T(8,128)(2,1)}, bf16[2,32,8,768]{3,2,1,0:T(8,128)(2,1)S(1)}, u32[]{:S(2)}, u32[]{:S(2)}) %collective-permute-start.3) | collective-permute-done | bytes 786464 | tf_op jit(solution)/shard_map/ppermute | solution.py:28
  42.1 3.0 %collective-permute-done.2 = bf16[2,32,8,768]{3,2,1,0:T(8,128)(2,1)} collective-permute-done((bf16[2,32,8,768]{3,2,1,0:T(8,128)(2,1)}, bf16[2,32,8,768]{3,2,1,0:T(8,128)(2,1)}, u32[]{:S(2)}, u32[]{:S(2)}) %collective-permute-start.2) | collective-permute-done | bytes 786464 | tf_op jit(solution)/shard_map/ppermute | solution.py:27
  45.1 1.3 pad_maximum_fusion
  46.7 1.5 gather_fusion.3
  48.2 1.5 gather_fusion.2
  49.7 2.5 broadcast_select_fusion.2
  52.2 2.7 reshape.774
  54.9 2.1 copy.37
  57.1 2.7 reshape.775
  59.8 2.1 copy.35
  61.9 1.8 bitcast_reduce_fusion
  65.4 1.3 multiply_reduce_fusion
  68.3 1.5 convolution_bitcast_fusion
  69.8 4.7 %copy.46 = f32[2,256,12,64]{3,2,1,0:T(8,128)} copy(f32[2,256,12,64]{1,3,2,0:T(8,128)} %convolution_bitcast_fusion) | data formatting | bytes 3145728 | tf_op jit(solution)/shard_map/nhqk,nqhd->nkhd/transpose | solution.py:140
  74.5 4.4 %reshape_reshape.37 = f32[8,49152]{1,0:T(8,128)} reshape(f32[2,256,12,64]{3,2,1,0:T(8,128)} %copy.46) | data formatting | bytes 3145728 | tf_op jit(solution)/shard_map/reshape;reshape | solution.py:149
  78.9 3.7 %copy.49 = f32[2,256,12,64]{3,2,1,0:T(8,128)} copy(f32[2,256,12,64]{1,3,2,0:T(8,128)S(1)} %convolution_bitcast_fusion.1) | data formatting | bytes 3145728 | tf_op jit(solution)/shard_map/nhqk,nqhd->nkhd/transpose | solution.py:140
  82.7 4.6 %reshape_reshape.39 = f32[8,49152]{1,0:T(8,128)} reshape(f32[2,256,12,64]{3,2,1,0:T(8,128)} %copy.49) | data formatting | bytes 3145728 | tf_op jit(solution)/shard_map/reshape;reshape | solution.py:149
  87.2 3.4 %broadcast_select_fusion.1 = (f32[8,49152]{1,0:T(8,128)}, f32[8,49152]{1,0:T(8,128)}) fusion(f32[8,49152]{1,0:T(8,128)S(1)} %copy-done.4, pred[8]{0:T(512)(128)(4,1)S(1)} %get-tuple-element.142, f32[8,49152]{1,0:T(8,128)} %reshape_reshape.39), kind=kLoop, calls=%fused_computation.38 | loop fusion | flops 786432 | bytes 6291464 | tf_op jit(solution)/shard_map/jit(_where)/select_n | solution.py:150
  90.6 5.1 %scatter_custom_fusion.1 = f32[12,49152]{1,0:T(8,128)} fusion(s32[8]{0:T(128)} %fusion.33, f32[8,49152]{1,0:T(8,128)} %get-tuple-element.154, f32[]{:T(128)} %constant.347.clone.1), kind=kCustom, calls=%fused_computation.13 | custom fusion | flops 393216 | bytes 2359808 | tf_op jit(solution)/shard_map/scatter-add | solution.py:152
  95.7 2.0 convert.17
  98.2 4.9 %scatter_custom_fusion = f32[12,49152]{1,0:T(8,128)} fusion(s32[8]{0:T(128)} %fusion.33, f32[8,49152]{1,0:T(8,128)} %get-tuple-element.153, f32[]{:T(128)} %constant.347.clone.1), kind=kCustom, calls=%fused_computation.15 | custom fusion | flops 393216 | bytes 2359808 | tf_op jit(solution)/shard_map/scatter-add | solution.py:152
  103.1 2.0 convert.16
  106.8 1.4 collective-permute-start.5
  108.9 1.2 copy.38
  110.0 1.9 reshape_reshape.35
  111.9 2.9 %fusion.19 = f32[768,768]{1,0:T(8,128)} fusion(bf16[128,768]{0,1:T(8,128)(2,1)} %reshape_reshape.35, bf16[16,8,768]{2,1,0:T(8,128)(2,1)} %param.32), kind=kOutput, calls=%fused_computation.71 | convolution fusion | flops 150994944 | bytes 2752512 | tf_op jit(solution)/shard_map/dot_general | solution.py:213
  114.9 8.5 %collective-permute-done.5 = bf16[2,8,24,768]{3,2,1,0:T(8,128)(2,1)} collective-permute-done((bf16[2,8,24,768]{3,2,1,0:T(8,128)(2,1)}, bf16[2,8,24,768]{3,2,1,0:T(8,128)(2,1)}, u32[]{:S(2)}, u32[]{:S(2)}) %collective-permute-start.5) | collective-permute-done | bytes 589856 | tf_op jit(solution)/shard_map/ppermute | solution.py:28
  123.4 7.5 %collective-permute-done.4 = bf16[2,8,24,768]{3,2,1,0:T(8,128)(2,1)} collective-permute-done((bf16[2,8,24,768]{3,2,1,0:T(8,128)(2,1)}, bf16[2,8,24,768]{3,2,1,0:T(8,128)(2,1)}, u32[]{:S(2)}, u32[]{:S(2)}) %collective-permute-start.4) | collective-permute-done | bytes 589856 | tf_op jit(solution)/shard_map/ppermute | solution.py:27
  130.8 2.9 %pad_maximum_fusion.4 = (bf16[2,48,8,768]{3,2,1,0:T(8,128)(2,1)}, bf16[2,48,8,768]{3,2,1,0:T(8,128)(2,1)}) fusion(bf16[2,8,24,768]{3,2,1,0:T(8,128)(2,1)} %collective-permute-done.5, bf16[2,8,24,768]{3,2,1,0:T(8,128)(2,1)} %collective-permute-done.4, bf16[1,32,24,768]{3,2,1,0:T(8,128)(2,1)S(1)} %bitcast.90, bf16[1,32,24,768]{3,2,1,0:T(8,128)(2,1)S(1)} %bitcast.100), kind=kLoop, calls=%fused_computation.29 | loop fusion | flops 9437184 | bytes 5898240 | tf_op jit(solution)/shard_map/slice | solution.py:25
  133.7 3.5 %collective-permute-start.7 = (bf16[2,48,8,768]{3,2,1,0:T(8,128)(2,1)}, bf16[2,48,8,768]{3,2,1,0:T(8,128)(2,1)}, u32[]{:S(2)}, u32[]{:S(2)}) collective-permute-start(bf16[2,48,8,768]{3,2,1,0:T(8,128)(2,1)} %get-tuple-element.144), channel_id=1, source_target_pairs={{1,0},{2,1},{3,2},{4,3},{5,4},{6,5},{7,6},{0,7},{9,8},{10,9},{11,1... | collective-permute-start | bytes 3538952 | tf_op jit(solution)/shard_map/ppermute | solution.py:28
  137.2 56.5 %all-reduce.3.cloned.1.call-done = f32[768,768]{1,0:T(8,128)} async-done(((f32[768,768]{1,0:T(8,128)}), f32[768,768]{1,0:T(8,128)}) %all-reduce.3.cloned.1.call-update) | async-done | bytes 2359312 | tf_op jit(solution)/shard_map/psum | solution.py:16
  193.8 2.5 fusion.9
  196.3 2.2 copy.44
  198.5 2.1 reshape_transpose_reshape_reshape.7
  200.5 2.0 fusion.10
  204.6 1.3 convert_add_fusion
  211.1 58.7 %all-reduce.5.cloned.1.call-done = f32[768,768]{1,0:T(8,128)} async-done(((f32[768,768]{1,0:T(8,128)}), f32[768,768]{1,0:T(8,128)}) %all-reduce.5.cloned.1.call-update) | async-done | bytes 2359312 | tf_op jit(solution)/shard_map/psum | solution.py:16
  269.8 3.2 %broadcast_multiply_fusion = f32[768,768]{1,0:T(8,128)} fusion(f32[768,768]{1,0:T(8,128)} %all-reduce.5.cloned.1.call-done), kind=kLoop, calls=%fused_computation.30 | loop fusion | flops 589824 | bytes 4718592 | tf_op jit(solution)/shard_map/div | solution.py:216
  (76 shorter events, 17.3 us)
Async XLA Ops:
  7.2 8.3 %copy-start = (bf16[768,768]{1,0:T(8,128)(2,1)S(1)}, bf16[768,768]{1,0:T(8,128)(2,1)}, u32[]{:S(2)}) copy-start(bf16[768,768]{1,0:T(8,128)(2,1)} %param.33) | copy-start | bytes 3538948
  7.2 14.6 %copy-start.7 = (bf16[16,8,768]{2,1,0:T(8,128)(2,1)S(1)}, bf16[16,8,768]{2,1,0:T(8,128)(2,1)}, u32[]{:S(2)}) copy-start(bf16[16,8,768]{2,1,0:T(8,128)(2,1)} %param.30) | copy-start | bytes 589828
  7.2 14.6 %copy-start.8 = (bf16[16,8,768]{2,1,0:T(8,128)(2,1)S(1)}, bf16[16,8,768]{2,1,0:T(8,128)(2,1)}, u32[]{:S(2)}) copy-start(bf16[16,8,768]{2,1,0:T(8,128)(2,1)} %param.31) | copy-start | bytes 589828
  7.2 186.6 %all-reduce.3.cloned.1.call-start = ((), (), s32[]{:S(2)}) async-start(), calls=%async_computation | async-start | bytes 4718592 | tf_op jit(solution)/shard_map/psum | solution.py:16
  8.4 9.3 %collective-permute-start.1 = (bf16[2,8,8,768]{3,2,1,0:T(8,128)(2,1)S(1)}, bf16[2,8,8,768]{3,2,1,0:T(8,128)(2,1)S(1)}, u32[]{:S(2)}, u32[]{:S(2)}) collective-permute-start(bf16[2,8,8,768]{3,2,1,0:T(8,128)(2,1)S(1)} %get-tuple-element.152), channel_id=1, source_target_pairs={{8,0},{16,8},{24,16},{0,24},{9,1},{17,9},{25,17},{1,25},{10,2},{18... | collective-permute-start | bytes 589832 | tf_op jit(solution)/shard_map/ppermute | solution.py:28
  12.4 9.4 %collective-permute-start = (bf16[2,8,8,768]{3,2,1,0:T(8,128)(2,1)S(1)}, bf16[2,8,8,768]{3,2,1,0:T(8,128)(2,1)S(1)}, u32[]{:S(2)}, u32[]{:S(2)}) collective-permute-start(bf16[2,8,8,768]{3,2,1,0:T(8,128)(2,1)S(1)} %get-tuple-element.151), channel_id=1, source_target_pairs={{0,8},{8,16},{16,24},{24,0},{1,9},{9,17},{17,25},{25,1},{2,10},{10... | collective-permute-start | bytes 589832 | tf_op jit(solution)/shard_map/ppermute | solution.py:27
  22.8 19.3 %collective-permute-start.3 = (bf16[2,32,8,768]{3,2,1,0:T(8,128)(2,1)}, bf16[2,32,8,768]{3,2,1,0:T(8,128)(2,1)S(1)}, u32[]{:S(2)}, u32[]{:S(2)}) collective-permute-start(bf16[2,32,8,768]{3,2,1,0:T(8,128)(2,1)} %pad_maximum_fusion.5), channel_id=1, source_target_pairs={{1,0},{2,1},{3,2},{4,3},{5,4},{6,5},{7,6},{0,7},{9,8},{10,9},{11,1... | collective-permute-start | bytes 2359304 | tf_op jit(solution)/shard_map/ppermute | solution.py:28
  24.9 20.1 %collective-permute-start.2 = (bf16[2,32,8,768]{3,2,1,0:T(8,128)(2,1)}, bf16[2,32,8,768]{3,2,1,0:T(8,128)(2,1)}, u32[]{:S(2)}, u32[]{:S(2)}) collective-permute-start(bf16[2,32,8,768]{3,2,1,0:T(8,128)(2,1)} %pad_maximum_fusion.5), channel_id=1, source_target_pairs={{0,1},{1,2},{2,3},{3,4},{4,5},{5,6},{6,7},{7,0},{8,9},{9,10},{10,1... | collective-permute-start | bytes 2359304 | tf_op jit(solution)/shard_map/ppermute | solution.py:27
  48.2 1.5 copy-start.6
  61.9 2.4 copy-start.3
  64.3 1.1 copy-start.2
  66.7 1.6 copy-start.5
  67.4 0.9 copy-start.1
  82.7 4.6 %copy-start.4 = (f32[8,49152]{1,0:T(8,128)S(1)}, f32[8,49152]{1,0:T(8,128)}, u32[]{:S(2)}) copy-start(f32[8,49152]{1,0:T(8,128)} %reshape_reshape.37) | copy-start | bytes 4718596
  105.7 3.2 %copy-start.9 = (bf16[2,64,12,64]{1,3,2,0:T(8,128)(2,1)S(1)}, bf16[2,64,12,64]{1,3,2,0:T(8,128)(2,1)}, u32[]{:S(2)}) copy-start(bf16[2,64,12,64]{1,3,2,0:T(8,128)(2,1)} %get-tuple-element.162) | copy-start | bytes 589828
  106.8 16.5 %collective-permute-start.5 = (bf16[2,8,24,768]{3,2,1,0:T(8,128)(2,1)}, bf16[2,8,24,768]{3,2,1,0:T(8,128)(2,1)}, u32[]{:S(2)}, u32[]{:S(2)}) collective-permute-start(bf16[2,8,24,768]{3,2,1,0:T(8,128)(2,1)} %get-tuple-element.146), channel_id=1, source_target_pairs={{8,0},{16,8},{24,16},{0,24},{9,1},{17,9},{25,17},{1,25},{10,2},{18... | collective-permute-start | bytes 1769480 | tf_op jit(solution)/shard_map/ppermute | solution.py:28
  108.3 22.6 %collective-permute-start.4 = (bf16[2,8,24,768]{3,2,1,0:T(8,128)(2,1)}, bf16[2,8,24,768]{3,2,1,0:T(8,128)(2,1)}, u32[]{:S(2)}, u32[]{:S(2)}) collective-permute-start(bf16[2,8,24,768]{3,2,1,0:T(8,128)(2,1)} %get-tuple-element.145), channel_id=1, source_target_pairs={{0,8},{8,16},{16,24},{24,0},{1,9},{9,17},{17,25},{25,1},{2,10},{10... | collective-permute-start | bytes 1769480 | tf_op jit(solution)/shard_map/ppermute | solution.py:27
  114.8 154.9 %all-reduce.5.cloned.1.call-start = ((), (), s32[]{:S(2)}) async-start(), calls=%async_computation.1 | async-start | bytes 4718592 | tf_op jit(solution)/shard_map/psum | solution.py:16
  133.7 68.9 %collective-permute-start.7 = (bf16[2,48,8,768]{3,2,1,0:T(8,128)(2,1)}, bf16[2,48,8,768]{3,2,1,0:T(8,128)(2,1)}, u32[]{:S(2)}, u32[]{:S(2)}) collective-permute-start(bf16[2,48,8,768]{3,2,1,0:T(8,128)(2,1)} %get-tuple-element.144), channel_id=1, source_target_pairs={{1,0},{2,1},{3,2},{4,3},{5,4},{6,5},{7,6},{0,7},{9,8},{10,9},{11,1... | collective-permute-start | bytes 3538952 | tf_op jit(solution)/shard_map/ppermute | solution.py:28
  137.2 65.3 %collective-permute-start.6 = (bf16[2,48,8,768]{3,2,1,0:T(8,128)(2,1)}, bf16[2,48,8,768]{3,2,1,0:T(8,128)(2,1)}, u32[]{:S(2)}, u32[]{:S(2)}) collective-permute-start(bf16[2,48,8,768]{3,2,1,0:T(8,128)(2,1)} %get-tuple-element.143), channel_id=1, source_target_pairs={{0,1},{1,2},{2,3},{3,4},{4,5},{5,6},{6,7},{7,0},{8,9},{9,10},{10,1... | collective-permute-start | bytes 3538952 | tf_op jit(solution)/shard_map/ppermute | solution.py:27
Sparse Core Ops, SparseCore 0:
  114.9 78.7 all-reduce.2
  196.9 72.8 all-reduce.4
